TPU v7x, 32 devices: a whole 2x2x4 slice. The times are simulated.
32 devices in a mesh: row: 4 (over y, x), col: 4 (over z), depth: 2 (over core).
Axes of the slice: x: 2, y: 2, z: 4, core: 2. Of those that a mesh axis runs over, the one named last changes fastest.
Arguments:
- features: bfloat16 [4096, 768], P(('row', 'col', 'depth')), may hold values from -6 to 6
- w_value: bfloat16 [768, 3072], replicated, may hold values from -0.21875 to 0.21875
- att_src: bfloat16 [4, 768], replicated, may hold values from -12 to 12
- att_dst: bfloat16 [4, 768], replicated, may hold values from -0.3984375 to 0.3984375
- tile_cols: int32 [32, 8], P('row'), may hold values from 0 to 31, as said below
- tile_count: int32 [32], P('row'), may hold values from 2 to 8, as said below
- neighbours: int32 [4096, 16], P('row'), may hold values from 0 to 4095, as said below
Outputs:
- mixed: bfloat16 [4096, 768], P(('row', 'col', 'depth'))
Inputs may be any that keep to these rules, and one draw needn't show every extreme that they name: tile_cols[t, 0] is t itself and the 8 tiles of a row tile are distinct. Tile c lies in run c // 2 and in column group (c // 2) % 4. Of the 8 tiles of one row tile at most 2 lie in one column group, and some row tile lists 2 of one group among its first tile_count tiles. Every tile of row tile t lies in t's run or in one of the 7 runs that follow it, cyclically over 16 runs, and some listed tile lies in the last of these. `tile_count`: some row tile lists all 8. The 16 neighbours of node i are distinct, differ from i, and lie in tiles tile_cols[i // 128, s] with s < tile_count[i // 128].
All inputs are finite; a program needn't handle non-finite values.
Results may differ from a plain program's by a relative error of at most 0.0059.
Values may be sent and summed in bfloat16 or wider, within the bound.
No kernel may reach another device: no remote copies, remote signals or barrier semaphores. Data moves between devices by JAX's collectives and lax.ppermute only.
A program may use at most 64 MiB of HBM per device.

v0:
```python
import jax
import jax.numpy as jnp
from jax import lax
from jax.sharding import PartitionSpec as P

D = 768
HEADS = 4
TILE = 128
SLOTS = 8
KNN = 16
GMAX = 2
LEAK_SLOPE = 0.2
NEG_BIG = -1e30


def from_behind(array, axis, by):
    length = lax.axis_size(axis)
    return lax.ppermute(array, axis, [(i, (i + by) % length) for i in range(length)])


def leaky_relu(inputs):
    return jnp.where(inputs > 0, inputs, LEAK_SLOPE * inputs)


def head_matrix(attention):
    heads_total, head_width = attention.shape
    selector = (jnp.arange(heads_total)[:, None] == jnp.arange(heads_total)[None, :]).astype(
        attention.dtype
    )
    spread = attention[:, :, None] * selector[:, None, :]
    return spread.reshape(heads_total * head_width, heads_total)


def project_rows(shard_rows, w_value):
    return jnp.dot(shard_rows, w_value, preferred_element_type=jnp.float32).astype(jnp.bfloat16)


def on_device(features, w_value, att_src, att_dst, tile_cols, tile_count, neighbours):
    source_matrix = head_matrix(att_src)
    target_matrix = head_matrix(att_dst)
    row_devices = lax.axis_size("row")
    col_devices = lax.axis_size("col")
    depth_devices = lax.axis_size("depth")
    own_row = lax.axis_index("row")
    own_col = lax.axis_index("col")
    own_depth = lax.axis_index("depth")
    piece_rows = features.shape[0]
    per_device = piece_rows // TILE
    block_tiles = tile_cols.shape[0]
    projected = [project_rows(features, w_value)]
    for distance in (1, 2):
        arrived = from_behind(features, "row", -distance)
        projected.append(project_rows(arrived, w_value))
    values = jnp.concatenate(projected, axis=0)
    own_values = projected[0]
    own_source = jnp.dot(own_values, source_matrix, preferred_element_type=jnp.float32)
    column_target = jnp.dot(values, target_matrix, preferred_element_type=jnp.float32)
    block_source = lax.all_gather(own_source, ("col", "depth"), axis=0, tiled=True)
    slot_index = jnp.arange(SLOTS, dtype=jnp.int32)
    run_index = tile_cols // (per_device * depth_devices)
    group_index = run_index % col_devices
    row_home = run_index // col_devices
    depth_home = tile_cols // per_device % depth_devices
    inside = (
        (group_index == own_col)
        & (depth_home == own_depth)
        & (slot_index[None, :] < tile_count[:, None])
    )
    local_tile = (row_home - own_row) % row_devices * per_device + tile_cols % per_device
    ranking = jnp.cumsum(inside.astype(jnp.int32), axis=1) - 1
    choose = inside[:, None, :] & (
        ranking[:, None, :] == jnp.arange(GMAX, dtype=jnp.int32)[None, :, None]
    )
    present = jnp.any(choose, axis=2)
    chosen_tile = jnp.sum(jnp.where(choose, tile_cols[:, None, :], 0), axis=2)
    chosen_local = jnp.sum(jnp.where(choose, local_tile[:, None, :], 0), axis=2)
    row_tiles = own_row * block_tiles + jnp.arange(block_tiles, dtype=jnp.int32)
    value_tiles = values.reshape(-1, TILE, HEADS * D)
    target_tiles = column_target.reshape(-1, TILE, HEADS)
    source_tiles = block_source.reshape(block_tiles, TILE, HEADS)
    near_tiles = neighbours.reshape(block_tiles, TILE, KNN)
    column_pos = jnp.arange(TILE, dtype=jnp.int32)

    def tile_logits(source, near_ids, pick_tile, pick_local, pick_live, home_tile):
        target = jnp.transpose(target_tiles[pick_local], (2, 0, 1)).reshape(HEADS, 1, GMAX * TILE)
        logits = leaky_relu(jnp.transpose(source)[:, :, None] + target)
        near_tile = near_ids // TILE
        near_spot = near_ids % TILE
        tile_hit = near_tile[:, :, None] == pick_tile[None, None, :]
        spot_hit = near_spot[:, :, None] == column_pos[None, None, :]
        linked = jnp.any(tile_hit[:, :, :, None] & spot_hit[:, :, None, :], axis=1)
        itself = (pick_tile == home_tile)[None, :, None] & (
            column_pos[:, None, None] == column_pos[None, None, :]
        )
        linked = ((linked | itself) & pick_live[None, :, None]).reshape(TILE, GMAX * TILE)
        return (jnp.where(linked[None], logits, NEG_BIG), linked)

    tile_inputs = (source_tiles, near_tiles, chosen_tile, chosen_local, present, row_tiles)

    def local_stats(inputs):
        logits, linked = tile_logits(
            inputs[0], inputs[1], inputs[2], inputs[3], inputs[4], inputs[5]
        )
        row_max = jnp.max(logits, axis=2)
        weights = jnp.where(linked[None], jnp.exp(logits - row_max[:, :, None]), 0.0)
        return (row_max, jnp.sum(weights, axis=2))

    local_max, local_sum = lax.map(local_stats, tile_inputs)
    global_peak = lax.pmax(local_max.astype(jnp.bfloat16), ("col", "depth")).astype(local_max.dtype)
    global_total = lax.psum(local_sum * jnp.exp(local_max - global_peak), ("col", "depth"))

    def tile_mix(inputs):
        logits, linked = tile_logits(
            inputs[0], inputs[1], inputs[2], inputs[3], inputs[4], inputs[5]
        )
        tile_peak = inputs[6]
        tile_total = inputs[7]
        scaled = jnp.exp(logits - tile_peak[:, :, None]) / tile_total[:, :, None]
        weights = jnp.where(linked[None], scaled, 0.0).astype(jnp.bfloat16)
        gathered = value_tiles[inputs[3]].reshape(GMAX * TILE, HEADS, D)
        return jnp.einsum("hij,jhd->id", weights, gathered, preferred_element_type=jnp.float32)

    partial_sums = lax.map(tile_mix, tile_inputs + (global_peak, global_total)).reshape(
        block_tiles * TILE, D
    )
    mixed_rows = lax.psum_scatter(partial_sums, ("col", "depth"), scatter_dimension=0, tiled=True)
    return jax.nn.elu(mixed_rows / HEADS).astype(jnp.bfloat16)


def solution(mesh):
    placed = (
        P(("row", "col", "depth"), None),
        P(),
        P(),
        P(),
        P("row", None),
        P("row"),
        P("row", None),
    )
    return jax.shard_map(
        on_device,
        mesh=mesh,
        in_specs=placed,
        out_specs=P(("row", "col", "depth"), None),
        check_vma=False,
    )
```

profile of v0, /device:TPU:0, one launch (start us, length us, event | category | flops | bytes accessed | tf_op | source)
XLA Modules:
  0.0 234.0 jit_solution(7692492828668962442)
XLA Ops:
  6.5 3.1 %collective-permute-start.1 = (bf16[128,768]{1,0:T(8,128)(2,1)}, bf16[128,768]{1,0:T(8,128)(2,1)S(1)}, u32[]{:S(2)}, u32[]{:S(2)}) collective-permute-start(bf16[128,768]{1,0:T(8,128)(2,1)} %param.11), channel_id=1, source_target_pairs={{0,16},{8,24},{16,0},{24,8},{1,17},{9,25},{17,1},{25,9},{2,18},{10... | collective-permute-start | bytes 589832 | tf_op jit(solution)/shard_map/ppermute | solution.py:18
  9.6 1.4 collective-permute-start
  13.9 3.3 %convolution_convert_fusion.2 = bf16[128,3072]{1,0:T(8,128)(2,1)S(1)} fusion(bf16[128,768]{1,0:T(8,128)(2,1)} %param.11, bf16[768,3072]{1,0:T(8,128)(2,1)} %param.12), kind=kOutput, calls=%fused_computation.96 | convolution fusion | flops 604372992 | bytes 5701632 | tf_op jit(solution)/shard_map/dot_general | solution.py:35
  17.7 13.1 %all_gather.3 = f32[1024,4]{0,1:T(4,128)S(1)} all-gather(f32[128,4]{0,1:T(4,128)S(1)} %fusion.49), channel_id=1, replica_groups=mesh['row'=4,'col'=4,'depth'=2] {'col','depth'}, dimensions={0}, use_global_device_ids=true | all-gather | bytes 18432 | tf_op jit(solution)/shard_map/all_gather | solution.py:58
  30.8 3.1 %convolution_convert_fusion = bf16[128,3072]{1,0:T(8,128)(2,1)S(1)} fusion(bf16[128,768]{1,0:T(8,128)(2,1)S(1)} %collective-permute-done.1, bf16[768,3072]{1,0:T(8,128)(2,1)} %param.12), kind=kOutput, calls=%fused_computation.94 | convolution fusion | flops 604372992 | bytes 5701632 | tf_op jit(solution)/shard_map/dot_general | solution.py:35
  35.0 1.4 copy-done.1
  37.1 37.4 %while.30 = (s32[]{:T(128)}, f32[8,4,128]{2,1,0:T(4,128)S(1)}, f32[8,4,128]{2,1,0:T(4,128)S(1)}, s32[8,128,16]{1,2,0:T(8,128)S(1)}, s32[8,2]{1,0:T(8,128)S(1)}, ...) while((s32[]{:T(128)}, f32[8,4,128]{2,1,0:T(4,128)S(1)}, ...), condition=%wide.region_8.9_spmd.clone.clone, body=%wide.region_4.8_spmd.clone.clone.sunk | while | flops 3282954 | bytes 990427 | solution.py:108
  39.0 1.0 and_reduce_fusion.4
  43.7 1.0 and_reduce_fusion.4
  48.4 1.0 and_reduce_fusion.4
  53.0 1.0 and_reduce_fusion.4
  57.7 1.0 and_reduce_fusion.4
  62.4 1.0 and_reduce_fusion.4
  67.1 1.0 and_reduce_fusion.4
  71.7 1.0 and_reduce_fusion.4
  74.6 15.9 %pmax.7 = bf16[8,4,128]{2,1,0:T(4,128)(2,1)S(1)} all-reduce(bf16[8,4,128]{2,1,0:T(4,128)(2,1)S(1)} %convert_element_type.42), channel_id=1, replica_groups=mesh['row'=4,'col'=4,'depth'=2] {'col','depth'}, use_global_device_ids=true, to_apply=%region_9.10 | all-reduce | flops 4096 | bytes 16384 | tf_op jit(solution)/shard_map/pmax | solution.py:109
  90.5 25.9 %psum.7 = f32[8,4,128]{2,1,0:T(4,128)S(1)} all-reduce(f32[8,4,128]{2,1,0:T(4,128)S(1)} %bitcast.208), channel_id=1, replica_groups=mesh['row'=4,'col'=4,'depth'=2] {'col','depth'}, use_global_device_ids=true, to_apply=%region_10.11 | all-reduce | flops 4096 | bytes 32768 | tf_op jit(solution)/shard_map/psum | solution.py:110
  116.4 71.1 %while.31 = (s32[]{:T(128)}, f32[8,128,768]{2,1,0:T(8,128)}, s32[8,128,16]{1,2,0:T(8,128)S(1)}, s32[8,2]{1,0:T(8,128)S(1)}, s32[8]{0:T(128)S(1)}, /*index=5*/pre...) while((s32[]{:T(128)}, f32[8,128,768]{2,1,0:T(8,128)}, ...), condition=%wide.region_13.14_spmd.clone.clone, body=%wide.region_11.13_spmd.clone.clone.sunk | while | flops 203955216 | bytes 9207539 | solution.py:123
  119.8 2.3 gather_fusion.1
  122.1 1.2 reshape.497
  124.0 1.3 fusion.97
  127.1 1.0 and_reduce_fusion.5
  128.7 2.3 gather_fusion.1
  131.0 1.2 reshape.497
  132.8 1.3 fusion.97
  136.0 1.0 and_reduce_fusion.5
  137.5 2.3 gather_fusion.1
  139.9 1.2 reshape.497
  141.7 1.3 fusion.97
  146.4 2.3 gather_fusion.1
  148.7 1.2 reshape.497
  150.6 1.4 fusion.97
  155.3 2.3 gather_fusion.1
  157.6 1.2 reshape.497
  159.5 1.3 fusion.97
  162.7 1.0 and_reduce_fusion.5
  164.2 2.3 gather_fusion.1
  166.5 1.2 reshape.497
  168.3 1.4 fusion.97
  173.1 2.3 gather_fusion.1
  175.4 1.2 reshape.497
  177.3 1.3 fusion.97
  180.4 1.0 and_reduce_fusion.5
  182.0 2.3 gather_fusion.1
  184.3 1.2 reshape.497
  186.1 1.3 fusion.97
  187.5 37.8 %reduce-scatter.2.cloned.1.call-done = f32[128,768]{1,0:T(8,128)} async-done(((f32[1024,768]{1,0:T(8,128)}), f32[128,768]{1,0:T(8,128)}) %reduce-scatter.2.cloned.1.call-update) | async-done | bytes 393232 | tf_op jit(solution)/shard_map/reduce_scatter | solution.py:126
  225.3 1.8 fusion.48
  (370 shorter events, 61.1 us)
Async XLA Ops:
  6.5 24.3 %copy-start = (s32[1024,16]{0,1:T(8,128)S(1)}, s32[1024,16]{0,1:T(8,128)}, u32[]{:S(2)}) copy-start(s32[1024,16]{0,1:T(8,128)} %param.17) | copy-start | bytes 196612
  6.5 10.7 %copy-start.3 = (bf16[4,768]{1,0:T(4,128)(2,1)S(1)}, bf16[4,768]{1,0:T(4,128)(2,1)}, u32[]{:S(2)}) copy-start(bf16[4,768]{1,0:T(4,128)(2,1)} %param.14) | copy-start | bytes 18436
  6.5 10.8 %copy-start.4 = (bf16[4,768]{1,0:T(4,128)(2,1)S(1)}, bf16[4,768]{1,0:T(4,128)(2,1)}, u32[]{:S(2)}) copy-start(bf16[4,768]{1,0:T(4,128)(2,1)} %param.13) | copy-start | bytes 18436
  6.5 218.8 %reduce-scatter.2.cloned.1.call-start = ((), (), s32[]{:S(2)}) async-start(), calls=%async_computation.1 | async-start | bytes 3538944 | tf_op jit(solution)/shard_map/reduce_scatter | solution.py:126
  6.5 24.3 %collective-permute-start.1 = (bf16[128,768]{1,0:T(8,128)(2,1)}, bf16[128,768]{1,0:T(8,128)(2,1)S(1)}, u32[]{:S(2)}, u32[]{:S(2)}) collective-permute-start(bf16[128,768]{1,0:T(8,128)(2,1)} %param.11), channel_id=1, source_target_pairs={{0,16},{8,24},{16,0},{24,8},{1,17},{9,25},{17,1},{25,9},{2,18},{10... | collective-permute-start | bytes 589832 | tf_op jit(solution)/shard_map/ppermute | solution.py:18
  9.6 24.4 %collective-permute-start = (bf16[128,768]{1,0:T(8,128)(2,1)}, bf16[128,768]{1,0:T(8,128)(2,1)S(1)}, u32[]{:S(2)}, u32[]{:S(2)}) collective-permute-start(bf16[128,768]{1,0:T(8,128)(2,1)} %param.11), channel_id=1, source_target_pairs={{0,24},{8,0},{16,8},{24,16},{1,25},{9,1},{17,9},{25,17},{2,26},{10... | collective-permute-start | bytes 589832 | tf_op jit(solution)/shard_map/ppermute | solution.py:18
  17.4 16.6 %copy-start.2 = (bf16[768,3072]{1,0:T(8,128)(2,1)S(1)}, bf16[768,3072]{1,0:T(8,128)(2,1)}, u32[]{:S(2)}) copy-start(bf16[768,3072]{1,0:T(8,128)(2,1)} %param.12) | copy-start | bytes 14155780
  35.0 1.4 copy-start.1
Sparse Core Ops, SparseCore 0:
  187.6 37.6 reduce-scatter.1
where the time goes:
time: 235 us; the launch traced here: 234 us
  local copies, waits for them, and re-layouts  57.5 us (24%)
  blocking collectives  55 us (23%)
  other arithmetic  44.9 us (19%)
  waiting for transfers between devices  37.8 us (16%)
  matrix products  18.9 us (8%)
  between operations  13.6 us (6%)
  starting transfers between devices  4.5 us (2%)
    reduce_scatter x1, waiting for transfers between devices, on_device(): lax.psum_scatter(partial_sums, ('col', 'depth'), scatter_dimension=0, til...  37.8 us
    psum x1, blocking collectives, on_device(): lax.psum(local_sum * jnp.exp(local_max - global_peak), ('col', 'depth'))  25.9 us
    gather x8, local copies, waits for them, and re-layouts, tile_mix(): gathered = value_tiles[inputs[3]].reshape(GMAX * TILE, HEADS, D)  18.5 us
    pmax x1, blocking collectives, on_device(): lax.pmax(local_max.astype(jnp.bfloat16), ('col', 'depth'))  15.9 us
    reduce_or x16, other arithmetic, tile_logits(): linked = jnp.any(tile_hit[:, :, :, None] & spot_hit[:, :, None, :], axis=1)  15.5 us
    all_gather x1, blocking collectives, on_device(): lax.all_gather(own_source, ('col', 'depth'), axis=0, tiled=True)  13.1 us
    dot_general x8, matrix products, tile_mix(): jnp.einsum('hij,jhd->id', weights, gathered, preferred_element_type=jnp.f...  10.8 us
    reshape x8, local copies, waits for them, and re-layouts, tile_mix(): gathered = value_tiles[inputs[3]].reshape(GMAX * TILE, HEADS, D)  9.83 us
  transfers between devices with their start and end apart: 3, of which 1 were waited for; matrix products, arithmetic and copies ran while one was open for 4% of the time, Pallas kernels for 0%

commit v1 on v0

--- a/solution.py
+++ b/solution.py
@@ -107,7 +107,8 @@
 
     local_max, local_sum = lax.map(local_stats, tile_inputs)
     global_peak = lax.pmax(local_max.astype(jnp.bfloat16), ("col", "depth")).astype(local_max.dtype)
-    global_total = lax.psum(local_sum * jnp.exp(local_max - global_peak), ("col", "depth"))
+    chunk = local_sum * jnp.exp(local_max - global_peak)
+    global_total = jnp.sum(lax.all_gather(chunk, ("col", "depth")), axis=0)
 
     def tile_mix(inputs):
         logits, linked = tile_logits(

time: 235 us -> 223 us (0.949)
  blocking collectives: 55 us -> 43 us
    psum x1 -> x0, blocking collectives: 25.9 us -> none  [on_device(): lax.psum(local_sum * jnp.exp(local_max - global_peak), ('col', 'depth'))]
    all_gather x0 -> x1, blocking collectives: none -> 14 us  [on_device(): global_total = jnp.sum(lax.all_gather(chunk, ('col', 'depth')), axis=0)]
where the time goes in v1:
time: 223 us; the launch traced here: 222 us
  local copies, waits for them, and re-layouts  57.5 us (26%)
  other arithmetic  45 us (20%)
  blocking collectives  43 us (19%)
  waiting for transfers between devices  37.9 us (17%)
  matrix products  19 us (9%)
  between operations  13.6 us (6%)
  starting transfers between devices  4.5 us (2%)
    reduce_scatter x1, waiting for transfers between devices, on_device(): lax.psum_scatter(partial_sums, ('col', 'depth'), scatter_dimension=0, til...  37.8 us
    gather x8, local copies, waits for them, and re-layouts, tile_mix(): gathered = value_tiles[inputs[3]].reshape(GMAX * TILE, HEADS, D)  18.5 us
    pmax x1, blocking collectives, on_device(): lax.pmax(local_max.astype(jnp.bfloat16), ('col', 'depth'))  15.9 us
    reduce_or x16, other arithmetic, tile_logits(): linked = jnp.any(tile_hit[:, :, :, None] & spot_hit[:, :, None, :], axis=1)  15.5 us
    all_gather x1, blocking collectives, on_device(): global_total = jnp.sum(lax.all_gather(chunk, ('col', 'depth')), axis=0)  14 us
    all_gather x1, blocking collectives, on_device(): lax.all_gather(own_source, ('col', 'depth'), axis=0, tiled=True)  13.1 us
    dot_general x8, matrix products, tile_mix(): jnp.einsum('hij,jhd->id', weights, gathered, preferred_element_type=jnp.f...  10.7 us
    reshape x8, local copies, waits for them, and re-layouts, tile_mix(): gathered = value_tiles[inputs[3]].reshape(GMAX * TILE, HEADS, D)  9.83 us
  transfers between devices with their start and end apart: 3, of which 1 were waited for; matrix products, arithmetic and copies ran while one was open for 4% of the time, Pallas kernels for 0%

profile of v1, /device:TPU:0, one launch (start us, length us, event | category | flops | bytes accessed | tf_op | source)
XLA Modules:
  0.0 222.2 jit_solution(16849581578967015308)
XLA Ops:
  6.5 3.1 %collective-permute-start.1 = (bf16[128,768]{1,0:T(8,128)(2,1)}, bf16[128,768]{1,0:T(8,128)(2,1)S(1)}, u32[]{:S(2)}, u32[]{:S(2)}) collective-permute-start(bf16[128,768]{1,0:T(8,128)(2,1)} %param.11), channel_id=1, source_target_pairs={{0,16},{8,24},{16,0},{24,8},{1,17},{9,25},{17,1},{25,9},{2,18},{10... | collective-permute-start | bytes 589832 | tf_op jit(solution)/shard_map/ppermute | solution.py:18
  9.6 1.4 collective-permute-start
  13.9 3.3 %convolution_convert_fusion.2 = bf16[128,3072]{1,0:T(8,128)(2,1)S(1)} fusion(bf16[128,768]{1,0:T(8,128)(2,1)} %param.11, bf16[768,3072]{1,0:T(8,128)(2,1)} %param.12), kind=kOutput, calls=%fused_computation.96 | convolution fusion | flops 604372992 | bytes 5701632 | tf_op jit(solution)/shard_map/dot_general | solution.py:35
  17.7 13.1 %all_gather.9 = f32[1024,4]{0,1:T(4,128)S(1)} all-gather(f32[128,4]{0,1:T(4,128)S(1)} %fusion.49), channel_id=1, replica_groups=mesh['row'=4,'col'=4,'depth'=2] {'col','depth'}, dimensions={0}, use_global_device_ids=true | all-gather | bytes 18432 | tf_op jit(solution)/shard_map/all_gather | solution.py:58
  30.8 3.2 %convolution_convert_fusion = bf16[128,3072]{1,0:T(8,128)(2,1)S(1)} fusion(bf16[128,768]{1,0:T(8,128)(2,1)S(1)} %collective-permute-done.1, bf16[768,3072]{1,0:T(8,128)(2,1)} %param.12), kind=kOutput, calls=%fused_computation.94 | convolution fusion | flops 604372992 | bytes 5701632 | tf_op jit(solution)/shard_map/dot_general | solution.py:35
  35.0 1.4 copy-done.1
  37.2 37.4 %while.30 = (s32[]{:T(128)}, f32[8,4,128]{2,1,0:T(4,128)S(1)}, f32[8,4,128]{2,1,0:T(4,128)S(1)}, s32[8,128,16]{1,2,0:T(8,128)S(1)}, s32[8,2]{1,0:T(8,128)S(1)}, ...) while((s32[]{:T(128)}, f32[8,4,128]{2,1,0:T(4,128)S(1)}, ...), condition=%wide.region_8.9_spmd.clone.clone, body=%wide.region_4.8_spmd.clone.clone.sunk | while | flops 3282954 | bytes 990427 | solution.py:108
  39.1 1.0 and_reduce_fusion.4
  43.7 1.0 and_reduce_fusion.4
  48.4 1.0 and_reduce_fusion.4
  53.1 1.0 and_reduce_fusion.4
  57.8 1.0 and_reduce_fusion.4
  62.4 1.0 and_reduce_fusion.4
  67.1 1.0 and_reduce_fusion.4
  71.8 1.0 and_reduce_fusion.4
  74.6 15.9 %pmax.7 = bf16[8,4,128]{2,1,0:T(4,128)(2,1)S(1)} all-reduce(bf16[8,4,128]{2,1,0:T(4,128)(2,1)S(1)} %convert_element_type.42), channel_id=1, replica_groups=mesh['row'=4,'col'=4,'depth'=2] {'col','depth'}, use_global_device_ids=true, to_apply=%region_9.10 | all-reduce | flops 4096 | bytes 16384 | tf_op jit(solution)/shard_map/pmax | solution.py:109
  90.6 14.0 %all-gather = f32[64,4,128]{2,1,0:T(4,128)S(1)} all-gather(f32[8,4,128]{2,1,0:T(4,128)S(1)} %bitcast.209), channel_id=2, replica_groups=mesh['row'=4,'col'=4,'depth'=2] {'col','depth'}, dimensions={0}, use_global_device_ids=true | all-gather | bytes 147456 | tf_op jit(solution)/shard_map/all_gather | solution.py:111
  104.6 71.1 %while.31 = (s32[]{:T(128)}, f32[8,128,768]{2,1,0:T(8,128)}, s32[8,128,16]{1,2,0:T(8,128)S(1)}, s32[8,2]{1,0:T(8,128)S(1)}, s32[8]{0:T(128)S(1)}, /*index=5*/pre...) while((s32[]{:T(128)}, f32[8,128,768]{2,1,0:T(8,128)}, ...), condition=%wide.region_13.14_spmd.clone.clone, body=%wide.region_11.13_spmd.clone.clone.sunk | while | flops 203955216 | bytes 9207539 | solution.py:124
  108.0 2.3 %gather_fusion.1 = bf16[2,128,3072]{2,1,0:T(8,128)(2,1)S(1)} fusion(bf16[3,128,3072]{2,1,0:T(8,128)(2,1)} %get-tuple-element.809, s32[1024]{0:T(1024)S(1)} %pad_clamp_fusion.5), kind=kCustom, calls=%fused_computation.2.clone.clone.1 | custom fusion | bytes 3145736 | tf_op jit(solution)/shard_map/while/body/eval_jaxpr/gather | solution.py:121
  110.3 1.2 reshape.498
  112.1 1.3 fusion.97
  116.8 2.3 %gather_fusion.1 = bf16[2,128,3072]{2,1,0:T(8,128)(2,1)S(1)} fusion(bf16[3,128,3072]{2,1,0:T(8,128)(2,1)} %get-tuple-element.809, s32[1024]{0:T(1024)S(1)} %pad_clamp_fusion.5), kind=kCustom, calls=%fused_computation.2.clone.clone.1 | custom fusion | bytes 3145736 | tf_op jit(solution)/shard_map/while/body/eval_jaxpr/gather | solution.py:121
  119.2 1.2 reshape.498
  121.0 1.3 fusion.97
  124.2 1.0 and_reduce_fusion.5
  125.7 2.3 %gather_fusion.1 = bf16[2,128,3072]{2,1,0:T(8,128)(2,1)S(1)} fusion(bf16[3,128,3072]{2,1,0:T(8,128)(2,1)} %get-tuple-element.809, s32[1024]{0:T(1024)S(1)} %pad_clamp_fusion.5), kind=kCustom, calls=%fused_computation.2.clone.clone.1 | custom fusion | bytes 3145736 | tf_op jit(solution)/shard_map/while/body/eval_jaxpr/gather | solution.py:121
  128.0 1.2 reshape.498
  129.9 1.3 fusion.97
  133.1 1.0 and_reduce_fusion.5
  134.6 2.3 %gather_fusion.1 = bf16[2,128,3072]{2,1,0:T(8,128)(2,1)S(1)} fusion(bf16[3,128,3072]{2,1,0:T(8,128)(2,1)} %get-tuple-element.809, s32[1024]{0:T(1024)S(1)} %pad_clamp_fusion.5), kind=kCustom, calls=%fused_computation.2.clone.clone.1 | custom fusion | bytes 3145736 | tf_op jit(solution)/shard_map/while/body/eval_jaxpr/gather | solution.py:121
  136.9 1.2 reshape.498
  138.7 1.4 fusion.97
  143.5 2.3 %gather_fusion.1 = bf16[2,128,3072]{2,1,0:T(8,128)(2,1)S(1)} fusion(bf16[3,128,3072]{2,1,0:T(8,128)(2,1)} %get-tuple-element.809, s32[1024]{0:T(1024)S(1)} %pad_clamp_fusion.5), kind=kCustom, calls=%fused_computation.2.clone.clone.1 | custom fusion | bytes 3145736 | tf_op jit(solution)/shard_map/while/body/eval_jaxpr/gather | solution.py:121
  145.8 1.2 reshape.498
  147.6 1.3 fusion.97
  150.8 1.0 and_reduce_fusion.5
  152.4 2.3 %gather_fusion.1 = bf16[2,128,3072]{2,1,0:T(8,128)(2,1)S(1)} fusion(bf16[3,128,3072]{2,1,0:T(8,128)(2,1)} %get-tuple-element.809, s32[1024]{0:T(1024)S(1)} %pad_clamp_fusion.5), kind=kCustom, calls=%fused_computation.2.clone.clone.1 | custom fusion | bytes 3145736 | tf_op jit(solution)/shard_map/while/body/eval_jaxpr/gather | solution.py:121
  154.7 1.2 reshape.498
  156.5 1.4 fusion.97
  159.7 1.0 and_reduce_fusion.5
  161.3 2.3 %gather_fusion.1 = bf16[2,128,3072]{2,1,0:T(8,128)(2,1)S(1)} fusion(bf16[3,128,3072]{2,1,0:T(8,128)(2,1)} %get-tuple-element.809, s32[1024]{0:T(1024)S(1)} %pad_clamp_fusion.5), kind=kCustom, calls=%fused_computation.2.clone.clone.1 | custom fusion | bytes 3145736 | tf_op jit(solution)/shard_map/while/body/eval_jaxpr/gather | solution.py:121
  163.6 1.2 reshape.498
  165.4 1.3 fusion.97
  170.1 2.3 %gather_fusion.1 = bf16[2,128,3072]{2,1,0:T(8,128)(2,1)S(1)} fusion(bf16[3,128,3072]{2,1,0:T(8,128)(2,1)} %get-tuple-element.809, s32[1024]{0:T(1024)S(1)} %pad_clamp_fusion.5), kind=kCustom, calls=%fused_computation.2.clone.clone.1 | custom fusion | bytes 3145736 | tf_op jit(solution)/shard_map/while/body/eval_jaxpr/gather | solution.py:121
  172.4 1.2 reshape.498
  174.3 1.3 fusion.97
  175.7 37.8 %reduce-scatter.2.cloned.1.call-done = f32[128,768]{1,0:T(8,128)} async-done(((f32[1024,768]{1,0:T(8,128)}), f32[128,768]{1,0:T(8,128)}) %reduce-scatter.2.cloned.1.call-update) | async-done | bytes 393232 | tf_op jit(solution)/shard_map/reduce_scatter | solution.py:127
  213.5 1.8 fusion.48
  (371 shorter events, 61.1 us)
Async XLA Ops:
  6.5 24.3 %copy-start = (s32[1024,16]{0,1:T(8,128)S(1)}, s32[1024,16]{0,1:T(8,128)}, u32[]{:S(2)}) copy-start(s32[1024,16]{0,1:T(8,128)} %param.17) | copy-start | bytes 196612
  6.5 10.7 %copy-start.3 = (bf16[4,768]{1,0:T(4,128)(2,1)S(1)}, bf16[4,768]{1,0:T(4,128)(2,1)}, u32[]{:S(2)}) copy-start(bf16[4,768]{1,0:T(4,128)(2,1)} %param.14) | copy-start | bytes 18436
  6.5 10.8 %copy-start.4 = (bf16[4,768]{1,0:T(4,128)(2,1)S(1)}, bf16[4,768]{1,0:T(4,128)(2,1)}, u32[]{:S(2)}) copy-start(bf16[4,768]{1,0:T(4,128)(2,1)} %param.13) | copy-start | bytes 18436
  6.5 206.9 %reduce-scatter.2.cloned.1.call-start = ((), (), s32[]{:S(2)}) async-start(), calls=%async_computation.1 | async-start | bytes 3538944 | tf_op jit(solution)/shard_map/reduce_scatter | solution.py:127
  6.5 24.3 %collective-permute-start.1 = (bf16[128,768]{1,0:T(8,128)(2,1)}, bf16[128,768]{1,0:T(8,128)(2,1)S(1)}, u32[]{:S(2)}, u32[]{:S(2)}) collective-permute-start(bf16[128,768]{1,0:T(8,128)(2,1)} %param.11), channel_id=1, source_target_pairs={{0,16},{8,24},{16,0},{24,8},{1,17},{9,25},{17,1},{25,9},{2,18},{10... | collective-permute-start | bytes 589832 | tf_op jit(solution)/shard_map/ppermute | solution.py:18
  9.6 24.4 %collective-permute-start = (bf16[128,768]{1,0:T(8,128)(2,1)}, bf16[128,768]{1,0:T(8,128)(2,1)S(1)}, u32[]{:S(2)}, u32[]{:S(2)}) collective-permute-start(bf16[128,768]{1,0:T(8,128)(2,1)} %param.11), channel_id=1, source_target_pairs={{0,24},{8,0},{16,8},{24,16},{1,25},{9,1},{17,9},{25,17},{2,26},{10... | collective-permute-start | bytes 589832 | tf_op jit(solution)/shard_map/ppermute | solution.py:18
  17.4 16.7 %copy-start.2 = (bf16[768,3072]{1,0:T(8,128)(2,1)S(1)}, bf16[768,3072]{1,0:T(8,128)(2,1)}, u32[]{:S(2)}) copy-start(bf16[768,3072]{1,0:T(8,128)(2,1)} %param.12) | copy-start | bytes 14155780
  35.0 1.4 copy-start.1
Sparse Core Ops, SparseCore 0:
  175.8 37.6 reduce-scatter.1
